TPU v7x, 32 devices: a whole 2x2x4 slice. The times are simulated.
32 devices in a mesh: cand: 16 (over z, x, core), tp: 2 (over y).
Axes of the slice: x: 2, y: 2, z: 4, core: 2. Of those that a mesh axis runs over, the one named last changes fastest.
Arguments:
- hidden_in: bfloat16 [128, 2, 8192], P('cand'), may hold values from -4 to 4
- queries: bfloat16 [128, 2, 32, 128], P('cand', None, 'tp'), may hold values from -128 to 128
- new_kv: bfloat16 [128, 2, 8, 2, 128], P('cand', None, 'tp'), may hold values from -5 to 5
- kv_cache: bfloat16 [128, 8, 2, 512, 128], P('cand', 'tp'), may hold values from -6 to 6
- lengths: int32 [128], P('cand'), may hold values from 128 to 512, as said below
- winner: int32 [8], replicated, may hold values from 0 to 15
- out_values: bfloat16 [4096, 8192], P('tp'), may hold values from -4 to 4
- out_scales: float32 [32, 64], P('tp'), may hold values from 0.008 to 0.032
Outputs:
- mixed: bfloat16 [128, 2, 8192], P('cand')
Inputs may be any that keep to these rules, and one draw needn't show every extreme that they name: `lengths`: every draw has some row with exactly 512 live slots.
All inputs are finite; a program needn't handle non-finite values.
Results may differ from a plain program's by a relative error of at most 0.013.
Values may be sent and summed in bfloat16 or wider, within the bound.
A program may use at most 128 MiB of HBM per device.

v0:
```python
import math
import jax
import jax.numpy as jnp
from jax import lax
from jax.sharding import PartitionSpec as P

BLOCK = 64
KB = 256


def own_blocks(cache_rows, row_lengths):

    def take_block(cache_row, row_length):
        return lax.dynamic_slice_in_dim(cache_row, row_length - BLOCK, BLOCK, 2)

    return jax.vmap(take_block)(cache_rows, row_lengths)


def local(hidden_in, queries, new_kv, kv_cache, lengths, winner, out_values, out_scales):
    problems = kv_cache.shape[0]
    kv_here = kv_cache.shape[1]
    steps_count = queries.shape[1]
    heads_here = queries.shape[2]
    head_dim = queries.shape[3]
    group = heads_here // kv_here
    blocks = own_blocks(kv_cache, lengths)
    owner_mask = winner == lax.axis_index("cand")
    masked = jnp.where(owner_mask[:, None, None, None, None], blocks, jnp.zeros((), jnp.bfloat16))
    forked = lax.psum(masked, "cand").astype(jnp.float32).astype(jnp.bfloat16)
    grouped = queries.reshape(problems, steps_count, kv_here, group, head_dim)
    factor = 1.0 / math.sqrt(head_dim)

    def scores_of(keys):
        return (
            jnp.einsum("ptkgd,pkjd->ptkgj", grouped, keys, preferred_element_type=jnp.float32)
            * factor
        )

    def combine_values(weights, values):
        return jnp.einsum("ptkgj,pkjd->ptkgd", weights, values, preferred_element_type=jnp.float32)

    fresh = jnp.transpose(new_kv, (0, 2, 3, 1, 4))
    fork_scores = scores_of(forked[:, :, 0])
    new_scores = scores_of(fresh[:, :, 0])
    causal = jnp.arange(steps_count)[None, :] <= jnp.arange(steps_count)[:, None]
    new_scores = jnp.where(causal[None, :, None, None, :], new_scores, -jnp.inf)
    live = lengths - BLOCK
    count = kv_cache.shape[3] // KB

    def block_scores(index):
        piece = lax.dynamic_slice_in_dim(kv_cache, index * KB, KB, 3)
        scores = scores_of(piece[:, :, 0])
        slots = index * KB + jnp.arange(KB, dtype=jnp.int32)
        valid = slots[None, :] < live[:, None]
        scores = jnp.where(valid[:, None, None, None, :], scores, -jnp.inf)
        return (scores, piece[:, :, 1])

    peak = jnp.maximum(jnp.max(fork_scores, -1), jnp.max(new_scores, -1))
    total = jnp.sum(jnp.exp(fork_scores - peak[..., None]), -1) + jnp.sum(
        jnp.exp(new_scores - peak[..., None]), -1
    )

    def first_pass(index, carry):
        peak_now, total_now = carry
        scores, unused_values = block_scores(index)
        higher = jnp.maximum(peak_now, jnp.max(scores, -1))
        total_now = total_now * jnp.exp(peak_now - higher) + jnp.sum(
            jnp.exp(scores - higher[..., None]), -1
        )
        return (higher, total_now)

    peak, total = lax.fori_loop(0, count, first_pass, (peak, total))

    def weigh(scores):
        return (jnp.exp(scores - peak[..., None]) / total[..., None]).astype(jnp.bfloat16)

    summed = combine_values(weigh(fork_scores), forked[:, :, 1]) + combine_values(
        weigh(new_scores), fresh[:, :, 1]
    )

    def second_pass(index, summed_now):
        scores, values = block_scores(index)
        return summed_now + combine_values(weigh(scores), values)

    summed = lax.fori_loop(0, count, second_pass, summed)
    attended = summed.astype(jnp.bfloat16).reshape(problems * steps_count, heads_here * head_dim)
    blocks_here = out_scales.shape[0]
    side = out_values.shape[0] // blocks_here
    width = out_values.shape[1]
    partial_terms = jnp.einsum(
        "rbk,bkn->rbn",
        attended.reshape(-1, blocks_here, side),
        out_values.reshape(blocks_here, side, width),
        preferred_element_type=jnp.float32,
    )
    spread = jnp.repeat(out_scales, side, axis=1)
    term = jnp.sum(partial_terms * spread[None], axis=1)
    residual = hidden_in.reshape(problems * steps_count, width)
    totals = lax.psum(term.astype(jnp.bfloat16), "tp").astype(jnp.float32)
    result = (residual.astype(jnp.float32) + totals).astype(jnp.bfloat16)
    return result.reshape(hidden_in.shape)


def solution(mesh):
    placed = (
        P("cand", None, None),
        P("cand", None, "tp", None),
        P("cand", None, "tp", None, None),
        P("cand", "tp", None, None, None),
        P("cand"),
        P(),
        P("tp", None),
        P("tp", None),
    )
    return jax.shard_map(
        local, mesh=mesh, in_specs=placed, out_specs=P("cand", None, None), check_vma=False
    )
```

profile of v0, /device:TPU:0, one launch (start us, length us, event | category | flops | bytes accessed | tf_op | source)
XLA Modules:
  0.0 181.5 jit_solution(16705224246081859264)
XLA Ops:
  6.5 12.2 %copy.17 = bf16[8,4,2,512,128]{4,1,2,0,3:T(4,128)(2,1)} copy(bf16[8,4,2,512,128]{4,3,2,1,0:T(8,128)(2,1)} %param.15) | data formatting | bytes 16777216 | tf_op args[3]
  18.7 5.0 %gather_fusion = bf16[8,4,2,64,128]{4,1,2,3,0:T(4,128)(2,1)S(1)} fusion(bf16[8,4,2,512,128]{4,1,2,0,3:T(4,128)(2,1)} %copy.17, s32[8]{0:T(128)S(1)} %fusion.42), kind=kCustom, calls=%fused_computation | custom fusion | bytes 2097312 | tf_op jit(solution)/shard_map/vmap()/gather | solution.py:14
  23.8 1.1 copy_select_fusion
  24.9 0.0 all-reduce.3.cloned.1.call-update
  25.0 0.0 all-reduce.5.cloned.1.call-start
  25.0 7.6 %copy.22 = bf16[8,4,2,512,128]{4,3,1,0,2:T(8,128)(2,1)} copy(bf16[8,4,2,512,128]{4,3,2,1,0:T(8,128)(2,1)} %param.15) | data formatting | bytes 16777216 | tf_op jit(solution)/shard_map/while | solution.py:72
  32.7 0.2 broadcast_in_dim.120
  32.9 0.3 copy.44
  33.2 0.7 fusion.45
  33.9 87.6 %all-reduce.3.cloned.1.call-done = bf16[8,4,2,64,128]{4,3,1,0,2:T(8,128)(2,1)} async-done(((bf16[8,4,2,64,128]{4,3,1,0,2:T(8,128)(2,1)}), bf16[8,4,2,64,128]{4,3,1,0,2:T(8,128)(2,1)}) %all-reduce.3.cloned.1.call-update) | async-done | bytes 1048592 | tf_op jit(solution)/shard_map/psum | solution.py:29
  121.5 1.5 fusion.44
  123.1 0.3 exponential_reduce_fusion.1
  123.4 0.1 exponential_reduce_fusion.2
  123.5 5.8 %while.28 = (s32[]{:T(128)}, f32[8,2,4,4]{3,1,2,0:T(2,128)S(1)}, f32[8,2,4,4]{3,1,2,0:T(2,128)S(1)}, s32[8]{0:T(128)S(1)}, bf16[8,4,2,512,128]{4,3,1,0,2:T(8,128...) while((s32[]{:T(128)}, f32[8,2,4,4]{3,1,2,0:T(2,128)S(1)}, ...), condition=%wide.region_8.9_spmd, body=%wide.region_5.8_spmd.sunk | while | flops 17107716 | bytes 2706619 | solution.py:72
  123.6 0.1 broadcast_compare_fusion.5
  123.6 2.4 %fusion.55 = (f32[8,2,4,4]{3,1,2,0:T(2,128)S(1)}, f32[8,2,4,4,256]{4,3,1,2,0:T(4,128)S(1)}) fusion(bf16[8,2,4,4,128]{4,3,1,2,0:T(4,128)(2,1)S(1)} %get-tuple-element.409, bf16[8,4,2,512,128]{4,3,1,0,2:T(8,128)(2,1)} %get-tuple-element.408, s32[]{:T(128)S(6)} %select_n.75, pred[8,256]{1,0:T(8,128)(4,1)S(1)} %broadcast_compare_fusion.5), kind=kOutput, calls=%fused_computation.71.clone.1 | convolution fusion | flops 16973568 | bytes 2427908 | tf_op jit(solution)/shard_map/while/body/eval_jaxpr/ptkgd,pkjd->ptkgj/dot_general | solution.py:35
  126.1 0.3 exponential_reduce_fusion.4
  126.5 0.1 broadcast_compare_fusion.5
  126.5 2.4 %fusion.55 = (f32[8,2,4,4]{3,1,2,0:T(2,128)S(1)}, f32[8,2,4,4,256]{4,3,1,2,0:T(4,128)S(1)}) fusion(bf16[8,2,4,4,128]{4,3,1,2,0:T(4,128)(2,1)S(1)} %get-tuple-element.409, bf16[8,4,2,512,128]{4,3,1,0,2:T(8,128)(2,1)} %get-tuple-element.408, s32[]{:T(128)S(6)} %select_n.75, pred[8,256]{1,0:T(8,128)(4,1)S(1)} %broadcast_compare_fusion.5), kind=kOutput, calls=%fused_computation.71.clone.1 | convolution fusion | flops 16973568 | bytes 2427908 | tf_op jit(solution)/shard_map/while/body/eval_jaxpr/ptkgd,pkjd->ptkgj/dot_general | solution.py:35
  128.9 0.3 exponential_reduce_fusion.4
  129.3 0.3 convolution_bitcast_fusion.1
  129.6 0.3 fusion.28
  129.9 6.6 %while.29 = (s32[]{:T(128)}, f32[8,2,4,4,128]{4,3,1,2,0:T(4,128)S(1)}, bf16[8,4,2,512,128]{4,3,1,0,2:T(8,128)(2,1)}, s32[8]{0:T(128)S(1)}, bf16[8,2,4,4,128]{4,3...) while((s32[]{:T(128)}, ...), condition=%wide.region_10.11_spmd, body=%wide.region_9.10_spmd.sunk | while | flops 33917192 | bytes 4531923 | solution.py:85
  129.9 0.1 broadcast_compare_fusion.6
  130.0 3.2 %fusion.57 = f32[8,2,4,4,128]{4,3,1,2,0:T(4,128)S(1)} fusion(f32[8,2,4,4,128]{4,3,1,2,0:T(4,128)S(1)} %get-tuple-element.427, bf16[8,4,2,512,128]{4,3,1,0,2:T(8,128)(2,1)} %get-tuple-element.440, s32[]{:T(128)S(6)} %add.151, s32[]{:T(128)S(6)} %select_n.77, f32[8,2,4,4]{3,1,2,0:T(2,128)S(1)} %get-tuple-element.444, ...), kind=kOutput, calls=%fused_computation.23.clone.1 | convolution fusion | flops 33914880 | bytes 4527616 | tf_op jit(solution)/shard_map/while/body/eval_jaxpr/ptkgj,pkjd->ptkgd/dot_general | solution.py:40
  133.2 0.1 broadcast_compare_fusion.6
  133.3 3.2 %fusion.57 = f32[8,2,4,4,128]{4,3,1,2,0:T(4,128)S(1)} fusion(f32[8,2,4,4,128]{4,3,1,2,0:T(4,128)S(1)} %get-tuple-element.427, bf16[8,4,2,512,128]{4,3,1,0,2:T(8,128)(2,1)} %get-tuple-element.440, s32[]{:T(128)S(6)} %add.151, s32[]{:T(128)S(6)} %select_n.77, f32[8,2,4,4]{3,1,2,0:T(2,128)S(1)} %get-tuple-element.444, ...), kind=kOutput, calls=%fused_computation.23.clone.1 | convolution fusion | flops 33914880 | bytes 4527616 | tf_op jit(solution)/shard_map/while/body/eval_jaxpr/ptkgj,pkjd->ptkgd/dot_general | solution.py:40
  136.6 13.7 %fusion.27 = bf16[16,8192]{1,0:T(8,128)(2,1)} fusion(f32[16,8192]{1,0:T(8,128)S(1)} %bitcast.153, bf16[16,128,8192]{2,1,0:T(8,128)(2,1)} %bitcast.151, bf16[16,16,128]{2,1,0:T(8,128)(2,1)S(1)} %bitcast.159), kind=kOutput, calls=%fused_computation.36 | convolution fusion | flops 540934144 | bytes 34406400 | tf_op jit(solution)/shard_map/rbk,bkn->rbn/dot_general | solution.py:90
  150.2 0.1 reshape.97
  150.3 22.4 %all-reduce.5.cloned.1.call-done = bf16[16,8192]{1,0:T(8,128)(2,1)} async-done(((bf16[16,8192]{1,0:T(8,128)(2,1)}), bf16[16,8192]{1,0:T(8,128)(2,1)}) %all-reduce.5.cloned.1.call-update) | async-done | bytes 262160 | tf_op jit(solution)/shard_map/psum | solution.py:99
  172.8 1.0 add_convert_fusion
  173.8 0.9 reshape.96
  (36 shorter events, 0.3 us)
Async XLA Ops:
  6.5 115.0 %all-reduce.3.cloned.1.call-start = ((), (), s32[]{:S(2)}) async-start(), calls=%async_computation | async-start | bytes 2097152 | tf_op jit(solution)/shard_map/psum | solution.py:29
  6.5 12.2 %copy-start.6 = (s32[8]{0:T(128)S(1)}, s32[8]{0:T(128)}, u32[]{:S(2)}) copy-start(s32[8]{0:T(128)} %param.16) | copy-start | bytes 100
  6.5 17.2 %copy-start.5 = (s32[8]{0:T(128)S(1)}, s32[8]{0:T(128)}, u32[]{:S(2)}) copy-start(s32[8]{0:T(128)} %param.17) | copy-start | bytes 100
  24.9 7.7 %copy-start.1 = (bf16[8,2,16,128]{3,2,1,0:T(8,128)(2,1)S(1)}, bf16[8,2,16,128]{3,2,1,0:T(8,128)(2,1)}, u32[]{:S(2)}) copy-start(bf16[8,2,16,128]{3,2,1,0:T(8,128)(2,1)} %param.13) | copy-start | bytes 196612
  24.9 7.7 %copy-start.2 = (bf16[8,2,4,2,128]{4,3,2,1,0:T(2,128)(2,1)S(1)}, bf16[8,2,4,2,128]{4,3,2,1,0:T(2,128)(2,1)}, u32[]{:S(2)}) copy-start(bf16[8,2,4,2,128]{4,3,2,1,0:T(2,128)(2,1)} %param.14) | copy-start | bytes 98308
  24.9 7.7 %copy-start.3 = (f32[16,64]{1,0:T(8,128)S(1)}, f32[16,64]{1,0:T(8,128)}, u32[]{:S(2)}) copy-start(f32[16,64]{1,0:T(8,128)} %param.19) | copy-start | bytes 12292
  25.0 147.8 %all-reduce.5.cloned.1.call-start = ((), (), s32[]{:S(2)}) async-start(), calls=%async_computation.1 | async-start | bytes 524288 | tf_op jit(solution)/shard_map/psum | solution.py:99
  123.5 6.0 %copy-start.4 = (bf16[8,4,2,64,128]{4,3,1,0,2:T(8,128)(2,1)S(1)}, bf16[8,4,2,64,128]{4,3,1,0,2:T(8,128)(2,1)}, u32[]{:S(2)}) copy-start(bf16[8,4,2,64,128]{4,3,1,0,2:T(8,128)(2,1)} %all-reduce.3.cloned.1.call-done) | copy-start | bytes 3145732
  136.5 13.7 %copy-start = (bf16[8,2,8192]{2,1,0:T(2,128)(2,1)S(1)}, bf16[8,2,8192]{2,1,0:T(2,128)(2,1)}, u32[]{:S(2)}) copy-start(bf16[8,2,8192]{2,1,0:T(2,128)(2,1)} %param.12) | copy-start | bytes 786436
Sparse Core Ops, SparseCore 0:
  25.0 96.4 all-reduce.2
  150.4 22.3 all-reduce.4
where the time goes:
time: 182 us; the launch traced here: 181 us
  waiting for transfers between devices  110 us (60%)
  matrix products  27.6 us (15%)
  local copies, waits for them, and re-layouts  26.3 us (14%)
  between operations  13.6 us (7%)
  other arithmetic  3.67 us (2%)
    psum x1, waiting for transfers between devices, local(): forked = lax.psum(masked, 'cand').astype(jnp.float32).astype(jnp.bfloat16)  87.6 us
    psum x1, waiting for transfers between devices, local(): totals = lax.psum(term.astype(jnp.bfloat16), 'tp').astype(jnp.float32)  22.4 us
    dot_general x1, matrix products, local(): jnp.einsum('rbk,bkn->rbn', attended.reshape(-1, blocks_here, side), out_v...  13.7 us
    unnamed x17, local copies, waits for them, and re-layouts  12.5 us
    while x1, local copies, waits for them, and re-layouts, local(): peak, total = lax.fori_loop(0, count, first_pass, (peak, total))  7.6 us
    dot_general x4, matrix products, scores_of(): jnp.einsum('ptkgd,pkjd->ptkgj', grouped, keys, preferred_element_type=jnp...  6.99 us
    dot_general x4, matrix products, combine_values(): jnp.einsum('ptkgj,pkjd->ptkgd', weights, values, preferred_element_type=j...  6.96 us
    gather x1, local copies, waits for them, and re-layouts, take_block(): return lax.dynamic_slice_in_dim(cache_row, row_length - BLOCK, BLOCK, 2)  4.99 us
  transfers between devices with their start and end apart: 2, of which 2 were waited for; matrix products, arithmetic and copies ran while one was open for 5% of the time, Pallas kernels for 0%

commit v1 on v0

--- a/solution.py
+++ b/solution.py
@@ -26,7 +26,9 @@
     blocks = own_blocks(kv_cache, lengths)
     owner_mask = winner == lax.axis_index("cand")
     masked = jnp.where(owner_mask[:, None, None, None, None], blocks, jnp.zeros((), jnp.bfloat16))
-    forked = lax.psum(masked, "cand").astype(jnp.float32).astype(jnp.bfloat16)
+    forked = (
+        jnp.sum(lax.all_gather(masked, "cand"), axis=0).astype(jnp.float32).astype(jnp.bfloat16)
+    )
     grouped = queries.reshape(problems, steps_count, kv_here, group, head_dim)
     factor = 1.0 / math.sqrt(head_dim)
 

time: 182 us -> 223 us (1.23)
  waiting for transfers between devices: 110 us -> 142 us
  other arithmetic: 3.67 us -> 12.4 us
    all_gather x0 -> x1, waiting for transfers between devices: none -> 120 us  [local(): lax.all_gather(masked, 'cand')]
    psum x1 -> x0, waiting for transfers between devices: 87.6 us -> none  [local(): forked = lax.psum(masked, 'cand').astype(jnp.float32).astype(jnp.bfloat16)]
    reduce_sum x0 -> x1, other arithmetic: none -> 9.34 us  [local(): jnp.sum(lax.all_gather(masked, 'cand'), axis=0).astype(jnp.float32)]
    unnamed x17 -> x16, local copies, waits for them, and re-layouts: 12.5 us -> 12.6 us
  transfers between devices with their start and end apart: 2 -> 2, of which waited for: 2 -> 2; matrix products, arithmetic and copies ran while one was open for 5% -> 4% of each run, Pallas kernels for 0% -> 0%
where the time goes in v1:
time: 223 us; the launch traced here: 222 us
  waiting for transfers between devices  142 us (64%)
  local copies, waits for them, and re-layouts  27.7 us (12%)
  matrix products  26.5 us (12%)
  between operations  13.6 us (6%)
  other arithmetic  12.4 us (6%)
    all_gather x1, waiting for transfers between devices, local(): lax.all_gather(masked, 'cand')  120 us
    psum x1, waiting for transfers between devices, local(): totals = lax.psum(term.astype(jnp.bfloat16), 'tp').astype(jnp.float32)  21.5 us
    dot_general x1, matrix products, local(): jnp.einsum('rbk,bkn->rbn', attended.reshape(-1, blocks_here, side), out_v...  13.7 us
    unnamed x16, local copies, waits for them, and re-layouts  12.6 us
    reduce_sum x1, other arithmetic, local(): jnp.sum(lax.all_gather(masked, 'cand'), axis=0).astype(jnp.float32)  9.34 us
    while x1, local copies, waits for them, and re-layouts, local(): peak, total = lax.fori_loop(0, count, first_pass, (peak, total))  7.6 us
    dot_general x4, matrix products, combine_values(): jnp.einsum('ptkgj,pkjd->ptkgd', weights, values, preferred_element_type=j...  6.95 us
    dot_general x4, matrix products, scores_of(): jnp.einsum('ptkgd,pkjd->ptkgj', grouped, keys, preferred_element_type=jnp...  5.88 us
  transfers between devices with their start and end apart: 2, of which 2 were waited for; matrix products, arithmetic and copies ran while one was open for 4% of the time, Pallas kernels for 0%

profile of v1, /device:TPU:0, one launch (start us, length us, event | category | flops | bytes accessed | tf_op | source)
XLA Modules:
  0.0 222.2 jit_solution(18076443242618523915)
XLA Ops:
  6.5 12.2 %copy.35 = bf16[8,4,2,512,128]{4,1,2,0,3:T(4,128)(2,1)} copy(bf16[8,4,2,512,128]{4,3,2,1,0:T(8,128)(2,1)} %param.15) | data formatting | bytes 16777216 | tf_op args[3]
  18.7 5.0 %gather_fusion = bf16[8,4,2,64,128]{4,1,2,3,0:T(4,128)(2,1)S(1)} fusion(bf16[8,4,2,512,128]{4,1,2,0,3:T(4,128)(2,1)} %copy.35, s32[8]{0:T(128)S(1)} %fusion.40), kind=kCustom, calls=%fused_computation | custom fusion | bytes 2097312 | tf_op jit(solution)/shard_map/vmap()/gather | solution.py:14
  23.8 0.5 bitcast_select_fusion
  24.3 1.4 copy.36
  25.7 7.6 %copy.44 = bf16[8,4,2,512,128]{4,3,1,0,2:T(8,128)(2,1)} copy(bf16[8,4,2,512,128]{4,3,2,1,0:T(8,128)(2,1)} %param.15) | data formatting | bytes 16777216 | tf_op jit(solution)/shard_map/while | solution.py:74
  33.4 0.2 broadcast_in_dim.120
  33.6 0.3 copy.70
  34.0 0.7 fusion.43
  34.7 120.3 %all-gather.2.cloned.1.call-done = bf16[16,8,4,2,64,128]{5,4,3,2,1,0:T(8,128)(2,1)} async-done(((bf16[1,8,4,2,64,128]{5,4,3,2,1,0:T(8,128)(2,1)}), bf16[16,8,4,2,64,128]{5,4,3,2,1,0:T(8,128)(2,1)}) %all-gather.2.cloned.1.call-update) | async-done | bytes 16777232 | tf_op jit(solution)/shard_map/all_gather | solution.py:30
  155.0 9.3 %reduce_sum.52 = bf16[8,4,2,64,128]{4,3,2,1,0:T(8,128)(2,1)S(1)} reduce(bf16[16,8,4,2,64,128]{5,4,3,2,1,0:T(8,128)(2,1)} %all-gather.2.cloned.1.call-done, bf16[]{:T(256)} %constant.109.clone.1), dimensions={0}, to_apply=%region_0.1 | reduce | flops 7864320 | bytes 17825794 | tf_op jit(solution)/shard_map/reduce_sum | solution.py:30
  164.3 0.5 fusion.42
  164.8 0.3 exponential_reduce_fusion.1
  165.1 0.1 exponential_reduce_fusion.2
  165.3 5.7 %while.28 = (s32[]{:T(128)}, f32[8,2,4,4]{3,1,2,0:T(2,128)S(1)}, f32[8,2,4,4]{3,1,2,0:T(2,128)S(1)}, s32[8]{0:T(128)S(1)}, bf16[8,4,2,512,128]{4,3,1,0,2:T(8,128...) while((s32[]{:T(128)}, f32[8,2,4,4]{3,1,2,0:T(2,128)S(1)}, ...), condition=%wide.region_8.9_spmd, body=%wide.region_5.8_spmd.sunk | while | flops 17107716 | bytes 2706619 | solution.py:74
  165.3 0.1 broadcast_compare_fusion.5
  165.4 2.3 %fusion.54 = (f32[8,2,4,4]{3,1,2,0:T(2,128)S(1)}, f32[8,2,4,4,256]{4,3,1,2,0:T(4,128)S(1)}) fusion(bf16[8,2,4,4,128]{4,3,1,2,0:T(4,128)(2,1)S(1)} %get-tuple-element.435, bf16[8,4,2,512,128]{4,3,1,0,2:T(8,128)(2,1)} %get-tuple-element.434, s32[]{:T(128)S(6)} %select_n.82, pred[8,256]{1,0:T(8,128)(4,1)S(1)} %broadcast_compare_fusion.5), kind=kOutput, calls=%fused_computation.70.clone.1 | convolution fusion | flops 16973568 | bytes 2427908 | tf_op jit(solution)/shard_map/while/body/eval_jaxpr/ptkgd,pkjd->ptkgj/dot_general | solution.py:37
  167.8 0.3 exponential_reduce_fusion.4
  168.1 0.1 broadcast_compare_fusion.5
  168.2 2.3 %fusion.54 = (f32[8,2,4,4]{3,1,2,0:T(2,128)S(1)}, f32[8,2,4,4,256]{4,3,1,2,0:T(4,128)S(1)}) fusion(bf16[8,2,4,4,128]{4,3,1,2,0:T(4,128)(2,1)S(1)} %get-tuple-element.435, bf16[8,4,2,512,128]{4,3,1,0,2:T(8,128)(2,1)} %get-tuple-element.434, s32[]{:T(128)S(6)} %select_n.82, pred[8,256]{1,0:T(8,128)(4,1)S(1)} %broadcast_compare_fusion.5), kind=kOutput, calls=%fused_computation.70.clone.1 | convolution fusion | flops 16973568 | bytes 2427908 | tf_op jit(solution)/shard_map/while/body/eval_jaxpr/ptkgd,pkjd->ptkgj/dot_general | solution.py:37
  170.6 0.3 exponential_reduce_fusion.4
  171.0 0.3 convolution_bitcast_fusion.1
  171.2 0.3 fusion.26
  171.5 6.6 %while.29 = (s32[]{:T(128)}, f32[8,2,4,4,128]{4,3,1,2,0:T(4,128)S(1)}, bf16[8,4,2,512,128]{4,3,1,0,2:T(8,128)(2,1)}, s32[8]{0:T(128)S(1)}, bf16[8,2,4,4,128]{4,3...) while((s32[]{:T(128)}, ...), condition=%wide.region_10.11_spmd, body=%wide.region_9.10_spmd.sunk | while | flops 33917192 | bytes 4531923 | solution.py:87
  171.6 0.1 broadcast_compare_fusion.6
  171.6 3.2 %fusion.56 = f32[8,2,4,4,128]{4,3,1,2,0:T(4,128)S(1)} fusion(f32[8,2,4,4,128]{4,3,1,2,0:T(4,128)S(1)} %get-tuple-element.453, bf16[8,4,2,512,128]{4,3,1,0,2:T(8,128)(2,1)} %get-tuple-element.466, s32[]{:T(128)S(6)} %add.149, s32[]{:T(128)S(6)} %select_n.84, bf16[8,2,4,4,128]{4,3,1,2,0:T(4,128)(2,1)S(1)} %get-tuple-element.468, ...), kind=kOutput, calls=%fused_computation.23.clone.1 | convolution fusion | flops 33914880 | bytes 4527616 | tf_op jit(solution)/shard_map/while/body/eval_jaxpr/ptkgj,pkjd->ptkgd/dot_general | solution.py:42
  174.9 0.1 broadcast_compare_fusion.6
  174.9 3.2 %fusion.56 = f32[8,2,4,4,128]{4,3,1,2,0:T(4,128)S(1)} fusion(f32[8,2,4,4,128]{4,3,1,2,0:T(4,128)S(1)} %get-tuple-element.453, bf16[8,4,2,512,128]{4,3,1,0,2:T(8,128)(2,1)} %get-tuple-element.466, s32[]{:T(128)S(6)} %add.149, s32[]{:T(128)S(6)} %select_n.84, bf16[8,2,4,4,128]{4,3,1,2,0:T(4,128)(2,1)S(1)} %get-tuple-element.468, ...), kind=kOutput, calls=%fused_computation.23.clone.1 | convolution fusion | flops 33914880 | bytes 4527616 | tf_op jit(solution)/shard_map/while/body/eval_jaxpr/ptkgj,pkjd->ptkgd/dot_general | solution.py:42
  178.2 13.7 %fusion.25 = bf16[16,8192]{1,0:T(8,128)(2,1)} fusion(f32[16,8192]{1,0:T(8,128)S(1)} %bitcast.162, bf16[16,128,8192]{2,1,0:T(8,128)(2,1)} %bitcast.160, bf16[16,16,128]{2,1,0:T(8,128)(2,1)S(1)} %bitcast.168), kind=kOutput, calls=%fused_computation.35 | convolution fusion | flops 540934144 | bytes 34406400 | tf_op jit(solution)/shard_map/rbk,bkn->rbn/dot_general | solution.py:92
  191.9 0.1 reshape.104
  192.0 21.5 %all-reduce.2.cloned.1.call-done = bf16[16,8192]{1,0:T(8,128)(2,1)} async-done(((bf16[16,8192]{1,0:T(8,128)(2,1)}), bf16[16,8192]{1,0:T(8,128)(2,1)}) %all-reduce.2.cloned.1.call-update) | async-done | bytes 262160 | tf_op jit(solution)/shard_map/psum | solution.py:101
  213.5 1.0 add_convert_fusion
  214.5 0.9 reshape.103
  (37 shorter events, 0.4 us)
Async XLA Ops:
  6.5 148.4 %all-gather.2.cloned.1.call-start = ((), (), s32[]{:S(2)}) async-start(), calls=%async_computation | async-start | bytes 17825792 | tf_op jit(solution)/shard_map/all_gather | solution.py:30
  6.5 12.2 %copy-start.5 = (s32[8]{0:T(128)S(1)}, s32[8]{0:T(128)}, u32[]{:S(2)}) copy-start(s32[8]{0:T(128)} %param.16) | copy-start | bytes 100
  6.5 17.2 %copy-start.4 = (s32[8]{0:T(128)S(1)}, s32[8]{0:T(128)}, u32[]{:S(2)}) copy-start(s32[8]{0:T(128)} %param.17) | copy-start | bytes 100
  25.6 7.7 %copy-start.1 = (bf16[8,2,16,128]{3,2,1,0:T(8,128)(2,1)S(1)}, bf16[8,2,16,128]{3,2,1,0:T(8,128)(2,1)}, u32[]{:S(2)}) copy-start(bf16[8,2,16,128]{3,2,1,0:T(8,128)(2,1)} %param.13) | copy-start | bytes 196612
  25.7 7.7 %copy-start.2 = (bf16[8,2,4,2,128]{4,3,2,1,0:T(2,128)(2,1)S(1)}, bf16[8,2,4,2,128]{4,3,2,1,0:T(2,128)(2,1)}, u32[]{:S(2)}) copy-start(bf16[8,2,4,2,128]{4,3,2,1,0:T(2,128)(2,1)} %param.14) | copy-start | bytes 98308
  25.7 7.8 %copy-start.3 = (f32[16,64]{1,0:T(8,128)S(1)}, f32[16,64]{1,0:T(8,128)}, u32[]{:S(2)}) copy-start(f32[16,64]{1,0:T(8,128)} %param.19) | copy-start | bytes 12292
  25.7 187.8 %all-reduce.2.cloned.1.call-start = ((), (), s32[]{:S(2)}) async-start(), calls=%async_computation.1 | async-start | bytes 524288 | tf_op jit(solution)/shard_map/psum | solution.py:101
  178.2 13.7 %copy-start = (bf16[8,2,8192]{2,1,0:T(2,128)(2,1)S(1)}, bf16[8,2,8192]{2,1,0:T(2,128)(2,1)}, u32[]{:S(2)}) copy-start(bf16[8,2,8192]{2,1,0:T(2,128)(2,1)} %param.12) | copy-start | bytes 786436
Sparse Core Ops, SparseCore 0:
  25.8 129.1 all-gather.1
  192.0 21.4 all-reduce.1
